TPU v7x, 512 devices: a whole 4x4x16 slice. The times are simulated.
512 devices in a mesh: comp: 128 (over y, z, core), nest: 4 (over x).
Axes of the slice: x: 4, y: 4, z: 16, core: 2. Of those that a mesh axis runs over, the one named last changes fastest.
Arguments:
- spectra: bfloat16 [1152, 65536], P(None, ('nest', 'comp')), may hold values from 0.006 to 8.5, as said below
- kernel: bfloat16 [1152, 1152], replicated, may hold values from -0.1875 to 0.1875
- wind_gain: float32 [1152], replicated, may hold values from 0.02 to 0.3
- damping: float32 [1152], replicated, may hold values from 0.05 to 0.5
- wind_speed: float32 [65536], P(('nest', 'comp')), may hold values from 0.5 to 2
- class_speed: float32 [8, 32], replicated, may hold values from 0.15 to 0.65
- depth_class: int32 [4, 16384], P('nest'), may hold values from 0 to 7
- cell_of_point: int32 [4, 16384], P('nest'), may hold values from 0 to 16383, each once within a row
- sea_mask: int32 [256, 256], P('nest'), may hold values 0 or 1
- bnd_owner: int32 [4, 256], P('nest'), may hold values from 0 to 127
- bnd_slot: int32 [4, 256], P('nest'), may hold values from 0 to 127
Outputs:
- updated: bfloat16 [1152, 65536], P(None, ('nest', 'comp'))
- boundary: bfloat16 [4, 256, 1152], P('nest', 'comp')
Inputs may be any that keep to these rules, and one draw needn't show every extreme that they name: `spectra`: every entry is positive. `cell_of_point`: each row names every cell of its strip once.
All inputs are finite; a program needn't handle non-finite values. No bound on the sum of `sea_mask` on one device may be relied on, other than what follows from the above.
Results may differ from a plain program's by a relative error of at most 0.005.
Values may be sent and summed in bfloat16 or wider, within the bound.
A program may use at most 64 MiB of HBM per device.

v0:
```python
import math

import jax
import jax.numpy as jnp
from jax import lax
from jax.sharding import PartitionSpec as P

NDIR = 36


HIGHEST = lax.Precision.HIGHEST


def passed_along(value, axis, steps):
    count = lax.axis_size(axis)
    initial, last = (max(0, -steps), min(count, count - steps))
    return lax.ppermute(value, axis, [(source, source + steps) for source in range(initial, last)])


def body(
    spectra,
    kernel,
    wind_gain,
    damping,
    wind_speed,
    class_speed,
    depth_class,
    cell_of_point,
    sea_mask,
    bnd_owner,
    bnd_slot,
):
    comp_count, slot_count = spectra.shape
    group_size = lax.axis_size("comp")
    my_index = lax.axis_index("comp")
    per_device = comp_count // group_size
    strip_rows, strip_cols = sea_mask.shape
    cell_ids = cell_of_point[0]
    region_size = cell_ids.shape[0]
    sea_cells = sea_mask.astype(jnp.float32)
    fields = lax.all_to_all(spectra, "comp", split_axis=0, concat_axis=1, tiled=True)
    comp_ids = my_index * per_device + jnp.arange(per_device, dtype=jnp.int32)
    freq_ids = comp_ids // NDIR
    dir_ids = comp_ids % NDIR
    angles = dir_ids.astype(jnp.float32) * (2.0 * math.pi / NDIR)
    class_count, freq_count = class_speed.shape
    pick_freq = (freq_ids[:, None] == jnp.arange(freq_count, dtype=jnp.int32)[None, :]).astype(
        jnp.float32
    )
    speed_table = jnp.dot(pick_freq, class_speed.T, precision=HIGHEST)
    cell_class = jnp.zeros((region_size,), jnp.int32).at[cell_ids].set(depth_class[0])
    onehot = (jnp.arange(class_count, dtype=jnp.int32)[:, None] == cell_class[None, :]).astype(
        jnp.float32
    )
    speed = jnp.dot(speed_table, onehot, precision=HIGHEST).reshape(
        per_device, strip_rows, strip_cols
    )
    placed = jnp.zeros((per_device, region_size), jnp.bfloat16).at[:, cell_ids].set(fields)
    energy_field = (
        placed.astype(jnp.float32).reshape(per_device, strip_rows, strip_cols) * sea_cells
    )
    speed_x = speed * jnp.cos(angles)[:, None, None]
    speed_y = speed * jnp.sin(angles)[:, None, None]
    plus_x = jnp.maximum(speed_x, 0.0) * energy_field
    minus_x = jnp.minimum(speed_x, 0.0) * energy_field
    plus_y = jnp.maximum(speed_y, 0.0) * energy_field
    minus_y = jnp.minimum(speed_y, 0.0) * energy_field
    from_prev = passed_along(plus_x[:, -1, :], "nest", 1)
    from_next = passed_along(minus_x[:, 0, :], "nest", -1)
    inflow_x = jnp.concatenate([from_prev[:, None, :], plus_x[:, :-1]], 1) - jnp.concatenate(
        [minus_x[:, 1:], from_next[:, None, :]], 1
    )
    zero_column = jnp.zeros((per_device, strip_rows, 1), jnp.float32)
    inflow_y = jnp.concatenate([zero_column, plus_y[:, :, :-1]], 2) - jnp.concatenate(
        [minus_y[:, :, 1:], zero_column], 2
    )
    advected = (
        energy_field - (jnp.abs(speed_x) + jnp.abs(speed_y)) * energy_field + inflow_x + inflow_y
    ) * sea_cells
    advected_points = jnp.take(advected.reshape(per_device, region_size), cell_ids, axis=1).astype(
        jnp.bfloat16
    )
    owners = bnd_owner[0]
    slot_ids = bnd_slot[0]
    propagated = lax.all_to_all(advected_points, "comp", split_axis=1, concat_axis=0, tiled=True)
    owned = owners == my_index
    taken_rows = jnp.where(
        owned[:, None], jnp.take(propagated, slot_ids, axis=1).T.astype(jnp.float32), 0.0
    )
    boundary = lax.psum_scatter(taken_rows, "comp", scatter_dimension=0, tiled=True).astype(
        jnp.bfloat16
    )[None]
    first_point = my_index * slot_count
    my_cells = lax.dynamic_slice_in_dim(cell_ids, first_point, slot_count)
    live_mask = jnp.take(sea_cells.reshape(-1), my_cells)
    energy = jnp.sum(propagated, axis=0, dtype=jnp.float32) / comp_count
    forward = jnp.dot(kernel, propagated, preferred_element_type=jnp.float32)
    backward = lax.dot_general(
        kernel, propagated, (((0,), (0,)), ((), ())), preferred_element_type=jnp.float32
    )
    cross_terms = (forward * backward).astype(jnp.bfloat16)
    coupling = jnp.dot(kernel, cross_terms, preferred_element_type=jnp.float32)
    growth = 1.0 + wind_gain[:, None] * wind_speed[None, :] - damping[:, None] * energy[None, :]
    updated = (
        jnp.maximum(propagated.astype(jnp.float32) * growth + 0.1 * coupling, 0.0)
        * live_mask[None, :]
    ).astype(jnp.bfloat16)
    return (updated, boundary)


def solution(mesh):
    placed = (
        P(None, ("nest", "comp")),
        P(),
        P(),
        P(),
        P(("nest", "comp")),
        P(),
        P("nest", None),
        P("nest", None),
        P("nest", None),
        P("nest", None),
        P("nest", None),
    )
    return jax.shard_map(
        body,
        mesh=mesh,
        in_specs=placed,
        out_specs=(P(None, ("nest", "comp")), P("nest", "comp", None)),
        check_vma=False,
    )
```

profile of v0, /device:TPU:1, one launch (start us, length us, event | category | flops | bytes accessed | tf_op | source)
XLA Modules:
  0.0 782.3 jit_solution(14063455346922952181)
XLA Ops:
  0.7 2.0 all_to_all.26
  2.7 20.6 %all-to-all-start = ((bf16[128,9,128]{2,1,0:T(8,128)(2,1)}), bf16[128,9,128]{2,1,0:T(8,128)(2,1)S(1)}, u32[]{:S(2)}, u32[]{:S(2)}) async-start(bf16[128,9,128]{2,1,0:T(8,128)(2,1)} %all_to_all.26), calls=%async_computation | async-start | bytes 1048576 | tf_op jit(solution)/shard_map/all_to_all | solution.py:41
  25.1 60.6 %scatter_custom_fusion.1 = s32[16384]{0:T(1024)S(1)} fusion(s32[16384]{0:T(1024)S(1)} %bitcast.81, s32[16384]{0:T(1024)} %bitcast.89, s32[]{:T(128)} %constant.43.clone.1), kind=kCustom, calls=%fused_computation.39 | custom fusion | bytes 66048 | tf_op jit(solution)/shard_map/scatter | solution.py:51
  86.3 1.4 copy.52
  89.2 3.3 copy.40
  92.5 44.1 %scatter_custom_fusion = bf16[9,16384]{0,1:T(8,128)(2,1)} fusion(s32[16384]{0:T(1024)} %bitcast.83, bf16[16384,9]{1,0:T(8,128)(2,1)} %copy.40, bf16[]{:T(256)} %constant.52.clone.1), kind=kCustom, calls=%fused_computation.13 | custom fusion | bytes 295424 | tf_op jit(solution)/shard_map/scatter | solution.py:58
  136.6 3.7 copy.41
  141.5 1.3 slice_multiply_fusion.2
  142.9 3.1 collective-permute-start
  146.0 1.3 collective-permute-start.1
  147.8 2.7 collective-permute-done.1
  151.0 3.3 copy.44
  154.3 58.1 %gather_fusion = bf16[16384,9]{1,0:T(8,128)(2,1)} fusion(bf16[9,16384]{0,1:T(8,128)(2,1)} %bitcast.68, s32[16384]{0:T(1024)S(1)} %broadcast_clamp_fusion), kind=kCustom, calls=%fused_computation | custom fusion | bytes 655360 | tf_op jit(solution)/shard_map/jit(_take)/gather | solution.py:80
  212.5 3.8 copy.45
  217.2 17.8 %all-to-all-start.1 = ((bf16[9,128,128]{2,0,1:T(8,128)(2,1)}), bf16[9,128,128]{2,0,1:T(8,128)(2,1)S(1)}, u32[]{:S(2)}, u32[]{:S(2)}) async-start(bf16[9,128,128]{2,0,1:T(8,128)(2,1)} %select_convert_fusion), calls=%async_computation.1 | async-start | bytes 1048576 | tf_op jit(solution)/shard_map/all_to_all | solution.py:85
  235.1 1.3 dynamic-slice.1
  238.8 29.4 %all-to-all-done.1 = bf16[9,128,128]{2,0,1:T(8,128)(2,1)S(1)} async-done(((bf16[9,128,128]{2,0,1:T(8,128)(2,1)}), bf16[9,128,128]{2,0,1:T(8,128)(2,1)S(1)}, u32[]{:S(2)}, u32[]{:S(2)}) %all-to-all-start.1) | async-done | bytes 294944 | tf_op jit(solution)/shard_map/all_to_all | solution.py:85
  270.5 2.1 gather_fusion.2
  272.6 2.4 convert_select_fusion
  274.9 499.0 %all-reduce.4 = bf16[256,1152]{1,0:T(8,128)(2,1)} all-reduce(f32[256,1152]{1,0:T(8,128)} %convert_select_fusion), channel_id=2, replica_groups=mesh['comp'=128,'nest'=4] {'comp'}, use_global_device_ids=true, to_apply=%region_3.4.clone | all-reduce | flops 294912 | bytes 1769472
  774.0 1.8 fusion.25
  775.7 1.3 convert_reduce_fusion
  777.6 2.5 fusion.4
  781.0 1.3 fusion.16
  (57 shorter events, 12.4 us)
Async XLA Ops:
  0.6 773.3 %copy-start = (bf16[1152,1152]{1,0:T(8,128)(2,1)S(1)}, bf16[1152,1152]{1,0:T(8,128)(2,1)}, u32[]{:S(2)}) copy-start(bf16[1152,1152]{1,0:T(8,128)(2,1)} %param.12) | copy-start | bytes 7962628
  0.6 87.1 %copy-start.3 = (s32[1,16384]{1,0:T(1,128)S(1)}, s32[1,16384]{1,0:T(1,128)}, u32[]{:S(2)}) copy-start(s32[1,16384]{1,0:T(1,128)} %param.18) | copy-start | bytes 196612
  0.7 87.1 %copy-start.5 = (s32[64,256]{1,0:T(8,128)S(1)}, s32[64,256]{1,0:T(8,128)}, u32[]{:S(2)}) copy-start(s32[64,256]{1,0:T(8,128)} %param.19) | copy-start | bytes 196612
  2.7 86.0 %all-to-all-start = ((bf16[128,9,128]{2,1,0:T(8,128)(2,1)}), bf16[128,9,128]{2,1,0:T(8,128)(2,1)S(1)}, u32[]{:S(2)}, u32[]{:S(2)}) async-start(bf16[128,9,128]{2,1,0:T(8,128)(2,1)} %all_to_all.26), calls=%async_computation | async-start | bytes 1048576 | tf_op jit(solution)/shard_map/all_to_all | solution.py:41
  24.2 63.6 %copy-start.4 = (s32[16384,1]{0,1:T(1,128)}, s32[16384,1]{0,1:T(1,128)S(1)}, u32[]{:S(2)}) copy-start(s32[16384,1]{0,1:T(1,128)S(1)} %compare_select_fusion) | copy-start | bytes 196612
  141.5 9.0 %copy-start.1 = (f32[2,8,64,256]{3,2,1,0:T(8,128)S(1)}, f32[2,8,64,256]{3,2,1,0:T(8,128)}, u32[]{:S(2)}) copy-start(f32[2,8,64,256]{3,2,1,0:T(8,128)} %copy.52) | copy-start | bytes 3145732
  142.9 7.6 collective-permute-start
  146.0 4.5 collective-permute-start.1
  212.5 25.7 %copy-start.9 = (s32[1,256]{1,0:T(1,128)S(1)}, s32[1,256]{1,0:T(1,128)}, u32[]{:S(2)}) copy-start(s32[1,256]{1,0:T(1,128)} %param.21) | copy-start | bytes 3076
  212.5 25.8 %copy-start.8 = (s32[1,256]{1,0:T(1,128)S(1)}, s32[1,256]{1,0:T(1,128)}, u32[]{:S(2)}) copy-start(s32[1,256]{1,0:T(1,128)} %param.20) | copy-start | bytes 3076
  217.2 51.0 %all-to-all-start.1 = ((bf16[9,128,128]{2,0,1:T(8,128)(2,1)}), bf16[9,128,128]{2,0,1:T(8,128)(2,1)S(1)}, u32[]{:S(2)}, u32[]{:S(2)}) async-start(bf16[9,128,128]{2,0,1:T(8,128)(2,1)} %select_convert_fusion), calls=%async_computation.1 | async-start | bytes 1048576 | tf_op jit(solution)/shard_map/all_to_all | solution.py:85
  268.2 0.8 copy-start.2
  272.5 505.0 %copy-start.6 = (f32[1152]{0:T(1024)S(1)}, f32[1152]{0:T(1024)}, u32[]{:S(2)}) copy-start(f32[1152]{0:T(1024)} %param.14) | copy-start | bytes 13828
  272.5 505.0 %copy-start.7 = (f32[1152]{0:T(1024)S(1)}, f32[1152]{0:T(1024)}, u32[]{:S(2)}) copy-start(f32[1152]{0:T(1024)} %param.13) | copy-start | bytes 13828
where the time goes:
time: 787 us; the launch traced here: 782 us
  blocking collectives  499 us (63%)
  local copies, waits for them, and re-layouts  190 us (24%)
  starting transfers between devices  42.8 us (5%)
  waiting for transfers between devices  32.2 us (4%)
  other arithmetic  11 us (1%)
    unnamed x1, blocking collectives  499 us
    gather x2, local copies, waits for them, and re-layouts, body(): jnp.take(advected.reshape(per_device, region_size), cell_ids, axis=1)  61.9 us
    scatter x1, local copies, waits for them, and re-layouts, body(): jnp.zeros((region_size,), jnp.int32).at[cell_ids].set(depth_class[0])  60.6 us
    scatter x1, local copies, waits for them, and re-layouts, body(): jnp.zeros((per_device, region_size), jnp.bfloat16).at[:, cell_ids]  44.1 us
    all_to_all x1, waiting for transfers between devices, body(): lax.all_to_all(advected_points, 'comp', split_axis=1, concat_axis=0, tile...  29.4 us
    all_to_all x1, starting transfers between devices, body(): lax.all_to_all(spectra, 'comp', split_axis=0, concat_axis=1, tiled=True)  20.6 us
    all_to_all x1, starting transfers between devices, body(): lax.all_to_all(advected_points, 'comp', split_axis=1, concat_axis=0, tile...  17.8 us
  transfers between devices with their start and end apart: 4, of which 2 were waited for; matrix products, arithmetic and copies ran while one was open for 9% of the time, Pallas kernels for 0%

commit v1 on v0

--- a/solution.py
+++ b/solution.py
@@ -83,13 +83,11 @@
     owners = bnd_owner[0]
     slot_ids = bnd_slot[0]
     propagated = lax.all_to_all(advected_points, "comp", split_axis=1, concat_axis=0, tiled=True)
-    owned = owners == my_index
-    taken_rows = jnp.where(
-        owned[:, None], jnp.take(propagated, slot_ids, axis=1).T.astype(jnp.float32), 0.0
+    listed_cells = jnp.take(cell_ids, owners * slot_count + slot_ids)
+    listed = jnp.take(advected.reshape(per_device, region_size), listed_cells, axis=1).astype(
+        jnp.bfloat16
     )
-    boundary = lax.psum_scatter(taken_rows, "comp", scatter_dimension=0, tiled=True).astype(
-        jnp.bfloat16
-    )[None]
+    boundary = lax.all_to_all(listed, "comp", split_axis=1, concat_axis=0, tiled=True).T[None]
     first_point = my_index * slot_count
     my_cells = lax.dynamic_slice_in_dim(cell_ids, first_point, slot_count)
     live_mask = jnp.take(sea_cells.reshape(-1), my_cells)

time: 787 us -> 308 us (0.39)
  blocking collectives: 499 us -> 0 us
  waiting for transfers between devices: 32.2 us -> 45.7 us
    unnamed x1 -> x0, blocking collectives: 499 us -> none
    all_to_all x0 -> x1, starting transfers between devices: none -> 17.6 us  [body(): lax.all_to_all(listed, 'comp', split_axis=1, concat_axis=0, tiled=True)]
    all_to_all x0 -> x1, waiting for transfers between devices: none -> 14 us  [body(): lax.all_to_all(listed, 'comp', split_axis=1, concat_axis=0, tiled=True)]
    all_to_all x1, starting transfers between devices: 17.8 us -> 6.62 us  [body(): lax.all_to_all(advected_points, 'comp', split_axis=1, concat_axis=0, tile...]
  transfers between devices with their start and end apart: 4 -> 5, of which waited for: 2 -> 3; matrix products, arithmetic and copies ran while one was open for 9% -> 25% of each run, Pallas kernels for 0% -> 0%
where the time goes in v1:
time: 308 us; the launch traced here: 307 us
  local copies, waits for them, and re-layouts  194 us (63%)
  starting transfers between devices  49.4 us (16%)
  waiting for transfers between devices  45.7 us (15%)
  other arithmetic  9.96 us (3%)
  matrix products  6.82 us (2%)
    gather x2, local copies, waits for them, and re-layouts, body(): jnp.take(advected.reshape(per_device, region_size), cell_ids, axis=1)  61.9 us
    scatter x1, local copies, waits for them, and re-layouts, body(): jnp.zeros((region_size,), jnp.int32).at[cell_ids].set(depth_class[0])  60.6 us
    scatter x1, local copies, waits for them, and re-layouts, body(): jnp.zeros((per_device, region_size), jnp.bfloat16).at[:, cell_ids]  44.1 us
    all_to_all x1, waiting for transfers between devices, body(): lax.all_to_all(advected_points, 'comp', split_axis=1, concat_axis=0, tile...  29.1 us
    all_to_all x1, starting transfers between devices, body(): lax.all_to_all(spectra, 'comp', split_axis=0, concat_axis=1, tiled=True)  20.6 us
    all_to_all x1, starting transfers between devices, body(): lax.all_to_all(listed, 'comp', split_axis=1, concat_axis=0, tiled=True)  17.6 us
    all_to_all x1, waiting for transfers between devices, body(): lax.all_to_all(listed, 'comp', split_axis=1, concat_axis=0, tiled=True)  14 us
    all_to_all x1, starting transfers between devices, body(): lax.all_to_all(advected_points, 'comp', split_axis=1, concat_axis=0, tile...  6.62 us
  transfers between devices with their start and end apart: 5, of which 3 were waited for; matrix products, arithmetic and copies ran while one was open for 25% of the time, Pallas kernels for 0%

profile of v1, /device:TPU:1, one launch (start us, length us, event | category | flops | bytes accessed | tf_op | source)
XLA Modules:
  0.0 306.9 jit_solution(5044588795363510237)
XLA Ops:
  0.7 2.1 all_to_all.38
  2.7 20.6 %all-to-all-start = ((bf16[128,9,128]{2,1,0:T(8,128)(2,1)}), bf16[128,9,128]{2,1,0:T(8,128)(2,1)S(1)}, u32[]{:S(2)}, u32[]{:S(2)}) async-start(bf16[128,9,128]{2,1,0:T(8,128)(2,1)} %all_to_all.38), calls=%async_computation | async-start | bytes 1048576 | tf_op jit(solution)/shard_map/all_to_all | solution.py:41
  25.7 2.1 gather_fusion.2
  28.7 60.6 %scatter_custom_fusion.1 = s32[16384]{0:T(1024)S(1)} fusion(s32[16384]{0:T(1024)S(1)} %bitcast.91, s32[16384]{0:T(1024)} %bitcast.103, s32[]{:T(128)} %constant.55.clone.1), kind=kCustom, calls=%fused_computation.43 | custom fusion | bytes 66048 | tf_op jit(solution)/shard_map/scatter | solution.py:51
  89.2 1.6 fusion.11
  91.0 2.6 copy.55
  93.8 1.5 convert_bitcast_fusion
  95.9 3.3 %copy.43 = bf16[16384,9]{1,0:T(8,128)(2,1)} copy(bf16[16384,9]{0,1:T(8,128)(2,1)S(1)} %bitcast.88) | data formatting | bytes 589824 | tf_op jit(solution)/shard_map/all_to_all | solution.py:41
  99.2 44.1 %scatter_custom_fusion = bf16[9,16384]{0,1:T(8,128)(2,1)} fusion(s32[16384]{0:T(1024)S(1)} %bitcast.93, bf16[16384,9]{1,0:T(8,128)(2,1)} %copy.43, bf16[]{:T(256)} %constant.58.clone.1), kind=kCustom, calls=%fused_computation.14 | custom fusion | bytes 295424 | tf_op jit(solution)/shard_map/scatter | solution.py:58
  143.2 3.7 %copy.44 = f32[9,64,256]{2,1,0:T(8,128)S(1)} copy(bf16[9,64,256]{0,2,1:T(8,128)(2,1)} %bitcast.79) | data formatting | bytes 884736 | tf_op jit(solution)/shard_map/reshape | solution.py:60
  148.2 1.3 slice_multiply_fusion.2
  149.5 3.1 %collective-permute-start = (f32[9,256]{1,0:T(8,128)S(1)}, f32[9,256]{1,0:T(8,128)S(1)}, u32[]{:S(2)}, u32[]{:S(2)}) collective-permute-start(f32[9,256]{1,0:T(8,128)S(1)} %bitcast.96), channel_id=1, source_target_pairs={{0,1},{1,2},{2,3},{4,5},{5,6},{6,7},{8,9},{9,10},{10,11},{12,13},{... | collective-permute-start | bytes 27656 | tf_op jit(solution)/shard_map/ppermute | solution.py:17
  152.7 1.5 collective-permute-start.1
  154.6 2.6 collective-permute-done.1
  157.7 3.3 %copy.47 = bf16[9,64,256]{0,2,1:T(8,128)(2,1)} copy(bf16[9,64,256]{2,1,0:T(8,128)(2,1)S(1)} %fusion.10) | data formatting | bytes 589824 | tf_op jit(solution)/shard_map/mul | solution.py:77
  161.0 58.1 %gather_fusion = bf16[16384,9]{1,0:T(8,128)(2,1)} fusion(bf16[9,16384]{0,1:T(8,128)(2,1)} %bitcast.77, s32[16384]{0:T(1024)S(1)} %broadcast_clamp_fusion), kind=kCustom, calls=%fused_computation | custom fusion | bytes 655360 | tf_op jit(solution)/shard_map/jit(_take)/gather | solution.py:80
  219.1 3.7 %copy.48 = bf16[9,128,128]{2,0,1:T(8,128)(2,1)S(1)} copy(bf16[9,128,128]{0,2,1:T(8,128)(2,1)} %bitcast.83) | data formatting | bytes 589824 | tf_op jit(solution)/shard_map/jit(_take)/gather | solution.py:80
  222.8 3.5 %gather_fusion.3 = bf16[256,9]{1,0:T(8,128)(2,1)S(1)} fusion(bf16[9,16384]{0,1:T(8,128)(2,1)} %bitcast.78, s32[1024]{0:T(1024)S(1)} %pad_clamp_fusion), kind=kCustom, calls=%fused_computation.3 | custom fusion | bytes 10240 | tf_op jit(solution)/shard_map/jit(_take)/gather | solution.py:87
  227.1 17.6 %all-to-all-start.2 = ((bf16[9,128,2]{0,2,1:T(2,128)(2,1)}), bf16[9,128,2]{0,2,1:T(2,128)(2,1)S(1)}, u32[]{:S(2)}, u32[]{:S(2)}) async-start(bf16[9,128,2]{0,2,1:T(2,128)(2,1)} %select_convert_fusion.1), calls=%async_computation.2 | async-start | bytes 131072 | tf_op jit(solution)/shard_map/all_to_all | solution.py:90
  245.8 14.0 %all-to-all-done.2 = bf16[9,128,2]{0,2,1:T(2,128)(2,1)S(1)} async-done(((bf16[9,128,2]{0,2,1:T(2,128)(2,1)}), bf16[9,128,2]{0,2,1:T(2,128)(2,1)S(1)}, u32[]{:S(2)}, u32[]{:S(2)}) %all-to-all-start.2) | async-done | bytes 4640 | tf_op jit(solution)/shard_map/all_to_all | solution.py:90
  260.4 6.6 %all-to-all-start.1 = ((bf16[9,128,128]{2,0,1:T(8,128)(2,1)}), bf16[9,128,128]{2,0,1:T(8,128)(2,1)S(1)}, u32[]{:S(2)}, u32[]{:S(2)}) async-start(bf16[9,128,128]{2,0,1:T(8,128)(2,1)} %select_convert_fusion), calls=%async_computation.1 | async-start | bytes 1048576 | tf_op jit(solution)/shard_map/all_to_all | solution.py:85
  271.2 29.1 %all-to-all-done.1 = bf16[9,128,128]{2,0,1:T(8,128)(2,1)S(1)} async-done(((bf16[9,128,128]{2,0,1:T(8,128)(2,1)}), bf16[9,128,128]{2,0,1:T(8,128)(2,1)S(1)}, u32[]{:S(2)}, u32[]{:S(2)}) %all-to-all-start.1) | async-done | bytes 294944 | tf_op jit(solution)/shard_map/all_to_all | solution.py:85
  301.4 1.7 fusion.25
  303.4 2.6 fusion.4
  (57 shorter events, 15.1 us)
Async XLA Ops:
  0.6 300.7 %copy-start = (bf16[1152,1152]{1,0:T(8,128)(2,1)S(1)}, bf16[1152,1152]{1,0:T(8,128)(2,1)}, u32[]{:S(2)}) copy-start(bf16[1152,1152]{1,0:T(8,128)(2,1)} %param.12) | copy-start | bytes 7962628
  0.6 93.1 %copy-start.1 = (s32[1,16384]{1,0:T(1,128)S(1)}, s32[1,16384]{1,0:T(1,128)}, u32[]{:S(2)}) copy-start(s32[1,16384]{1,0:T(1,128)} %param.18) | copy-start | bytes 196612
  2.7 92.6 %all-to-all-start = ((bf16[128,9,128]{2,1,0:T(8,128)(2,1)}), bf16[128,9,128]{2,1,0:T(8,128)(2,1)S(1)}, u32[]{:S(2)}, u32[]{:S(2)}) async-start(bf16[128,9,128]{2,1,0:T(8,128)(2,1)} %all_to_all.38), calls=%async_computation | async-start | bytes 1048576 | tf_op jit(solution)/shard_map/all_to_all | solution.py:41
  148.2 9.0 %copy-start.2 = (f32[2,8,64,256]{3,2,1,0:T(8,128)S(1)}, f32[2,8,64,256]{3,2,1,0:T(8,128)}, u32[]{:S(2)}) copy-start(f32[2,8,64,256]{3,2,1,0:T(8,128)} %copy.55) | copy-start | bytes 3145732
  149.5 7.6 %collective-permute-start = (f32[9,256]{1,0:T(8,128)S(1)}, f32[9,256]{1,0:T(8,128)S(1)}, u32[]{:S(2)}, u32[]{:S(2)}) collective-permute-start(f32[9,256]{1,0:T(8,128)S(1)} %bitcast.96), channel_id=1, source_target_pairs={{0,1},{1,2},{2,3},{4,5},{5,6},{6,7},{8,9},{9,10},{10,11},{12,13},{... | collective-permute-start | bytes 27656 | tf_op jit(solution)/shard_map/ppermute | solution.py:17
  152.7 4.5 %collective-permute-start.1 = (f32[9,256]{1,0:T(8,128)S(1)}, f32[9,256]{1,0:T(8,128)S(1)}, u32[]{:S(2)}, u32[]{:S(2)}) collective-permute-start(f32[9,256]{1,0:T(8,128)S(1)} %bitcast.97), channel_id=1, source_target_pairs={{1,0},{2,1},{3,2},{5,4},{6,5},{7,6},{9,8},{10,9},{11,10},{13,12},{... | collective-permute-start | bytes 27656 | tf_op jit(solution)/shard_map/ppermute | solution.py:17
  227.1 32.6 %all-to-all-start.2 = ((bf16[9,128,2]{0,2,1:T(2,128)(2,1)}), bf16[9,128,2]{0,2,1:T(2,128)(2,1)S(1)}, u32[]{:S(2)}, u32[]{:S(2)}) async-start(bf16[9,128,2]{0,2,1:T(2,128)(2,1)} %select_convert_fusion.1), calls=%async_computation.2 | async-start | bytes 131072 | tf_op jit(solution)/shard_map/all_to_all | solution.py:90
  244.8 58.6 %copy-start.4 = (f32[1152]{0:T(1024)S(1)}, f32[1152]{0:T(1024)}, u32[]{:S(2)}) copy-start(f32[1152]{0:T(1024)} %param.14) | copy-start | bytes 13828
  244.8 58.6 %copy-start.5 = (f32[1152]{0:T(1024)S(1)}, f32[1152]{0:T(1024)}, u32[]{:S(2)}) copy-start(f32[1152]{0:T(1024)} %param.13) | copy-start | bytes 13828
  259.8 0.6 copy-start.3
  260.4 39.9 %all-to-all-start.1 = ((bf16[9,128,128]{2,0,1:T(8,128)(2,1)}), bf16[9,128,128]{2,0,1:T(8,128)(2,1)S(1)}, u32[]{:S(2)}, u32[]{:S(2)}) async-start(bf16[9,128,128]{2,0,1:T(8,128)(2,1)} %select_convert_fusion), calls=%async_computation.1 | async-start | bytes 1048576 | tf_op jit(solution)/shard_map/all_to_all | solution.py:85
  271.2 32.2 %copy-start.6 = (f32[128]{0:T(128)S(1)}, f32[128]{0:T(128)}, u32[]{:S(2)}) copy-start(f32[128]{0:T(128)} %fusion.21) | copy-start | bytes 1540

commit v2 on v1

v2 whole, which is shorter than its diff:
```python
import functools
import math

import jax
import jax.numpy as jnp
import numpy as np
from jax import lax
from jax.experimental import pallas as pl
from jax.experimental.pallas import tpu as pltpu
from jax.sharding import PartitionSpec as P

NDIR = 36
NESTED = 2
YDIM, ZDIM = 4, 16
F32, BF16, I32 = jnp.float32, jnp.bfloat16, jnp.int32


def nt(a, b):
    return lax.dot_general(a, b, (((1,), (1,)), ((), ())), preferred_element_type=F32)


def nn(a, b):
    return jnp.dot(a, b, preferred_element_type=F32)


def iota(shape, dim):
    return lax.broadcasted_iota(I32, shape, dim)


def onehot(mask):
    return jnp.where(mask, 1.0, 0.0).astype(BF16)


def step_kernel(
    sizes,
    spec_ref,
    kern_hbm,
    gain_ref,
    damp_ref,
    wind_ref,
    table_ref,
    cos_ref,
    sin_ref,
    class_ref,
    cell_ref,
    sea_ref,
    owner_ref,
    slot_ref,
    upd_ref,
    bnd_ref,
    lo_ref,
    hi_ref,
    cls_ref,
    col_ref,
    row_ref,
    colb_ref,
    rowb_ref,
    lhs_ref,
    acc_ref,
    adv_ref,
    advb_ref,
    last_s,
    main_r1,
    last_r1,
    main_s2,
    pair_s2,
    main_r2,
    pair_r2,
    bpt_ref,
    lastp_ref,
    listp_ref,
    halo_s,
    halo_r,
    prop_ref,
    kern_ref,
    kernt_ref,
    grow_ref,
    damp_b,
    cross_ref,
    kern_sem,
    s1_sem,
    r1_sem,
    s2_sem,
    r2_sem,
    halo_sem,
):
    nc, ncomp, pdev, srows, gy, nclass, nnest = sizes
    yd, zd = YDIM, ZDIM
    whole = 8 * nc
    span = yd * 2 * pdev
    me = lax.axis_index("comp")
    strip = lax.axis_index("nest")
    my_core = lax.rem(me, 2)
    my_z = lax.rem(me // 2, zd)
    my_y = me // (2 * zd)
    nxt = lax.rem(strip + 1, nnest)
    prv = lax.rem(strip + nnest - 1, nnest)

    def offset(j):
        odd = lax.rem(j, 2)
        return zd // 2 + odd * ((j + 1) // 2) - (1 - odd) * (j // 2)

    def chip_of(j, dy):
        return lax.rem(my_y - dy + yd, yd) * zd + lax.rem(my_z - offset(j) + 2 * zd, zd)

    def chip_to(j, dy):
        return lax.rem(my_y + dy, yd) * zd + lax.rem(my_z + offset(j), zd)

    def mirror(j):
        odd = lax.rem(j, 2)
        return j + odd * (1 - j // (zd - 1)) - (1 - odd) * ((j + zd - 1) // zd)

    kern_copy = pltpu.make_async_copy(kern_hbm, kern_ref, kern_sem)
    kern_copy.start()

    barrier = pltpu.get_barrier_semaphore()

    def greet(i, _):
        peer = lax.rem(me + i, nc)
        pl.semaphore_signal(barrier, inc=1, device_id={"comp": peer}, device_id_type=pl.DeviceIdType.MESH)
        return 0

    lax.fori_loop(1, nc, greet, 0)
    pl.semaphore_signal(barrier, inc=1, device_id={"nest": nxt}, device_id_type=pl.DeviceIdType.MESH)
    pl.semaphore_signal(barrier, inc=1, device_id={"nest": prv}, device_id_type=pl.DeviceIdType.MESH)

    tail = spec_ref[nc:, :, :].astype(F32).reshape(ncomp - whole, pdev)
    last_s[...] = tail.reshape(ncomp - whole, 1, pdev)
    cells = cell_ref[...]
    lo_ref[...] = jnp.bitwise_and(cells, gy - 1).astype(F32)
    hi_ref[...] = lax.shift_right_logical(cells, int(math.log2(gy))).astype(F32)
    cls_ref[...] = class_ref[...].astype(F32)

    def build(j, _):
        for dy in range(yd):
            for c in range(2):
                src = 2 * chip_of(j, dy) + c
                cols = pl.ds((2 * dy + c) * pdev, pdev)
                lo = lo_ref[pl.ds(src, 1), :]
                hi = hi_ref[pl.ds(src, 1), :]
                col_ref[j, :, cols] = onehot(iota((gy, pdev), 0).astype(F32) == lo)
                row_ref[j, :, cols] = onehot(iota((srows, pdev), 0).astype(F32) == hi)
        return 0

    lax.fori_loop(0, zd, build, 0)

    pl.semaphore_wait(barrier, nc - 1 + 2)

    def first(dest, j):
        pltpu.make_async_remote_copy(
            src_ref=spec_ref.at[dest],
            dst_ref=main_r1.at[me],
            send_sem=s1_sem.at[0],
            recv_sem=r1_sem.at[0, j],
            device_id={"comp": dest},
            device_id_type=pl.DeviceIdType.MESH,
        ).start()
        pltpu.make_async_remote_copy(
            src_ref=last_s.at[dest],
            dst_ref=last_r1.at[me],
            send_sem=s1_sem.at[1],
            recv_sem=r1_sem.at[1, j],
            device_id={"comp": dest},
            device_id_type=pl.DeviceIdType.MESH,
        ).start()

    def send_group(j, _):
        for dy in range(yd):
            for c in range(2):
                first(2 * chip_to(j, dy) + c, j)
        return 0

    lax.fori_loop(0, zd - 1, send_group, 0)
    for dy in range(1, yd):
        for c in range(2):
            first(2 * chip_to(zd - 1, dy) + c, zd - 1)
    first(me + 1 - 2 * my_core, zd - 1)
    main_r1[me] = spec_ref[me]
    last_r1[me] = last_s[me]

    owner_hot = onehot(iota((nc, NESTED * nc), 0) == owner_ref[...])
    slot_hot = iota((pdev, NESTED * nc), 0) == slot_ref[...]

    def listed(ref):
        by_slot = lax.dot_general(
            ref[...].astype(BF16), owner_hot, (((0,), (0,)), ((), ())), preferred_element_type=F32
        )
        return jnp.sum(jnp.where(slot_hot, by_slot, 0.0), axis=0, keepdims=True)

    colb_ref[...] = onehot(iota((gy, NESTED * nc), 0).astype(F32) == listed(lo_ref))
    rowb_ref[...] = onehot(iota((srows, NESTED * nc), 0).astype(F32) == listed(hi_ref))

    kern_copy.wait()
    blocks = ncomp // pdev

    def turn(i, _):
        for k in range(blocks):
            tile = kern_ref[pl.ds(pl.multiple_of(i * pdev, pdev), pdev), k * pdev : (k + 1) * pdev]
            kernt_ref[k * pdev : (k + 1) * pdev, pl.ds(pl.multiple_of(i * pdev, pdev), pdev)] = (
                tile.astype(F32).T.astype(BF16)
            )
        return 0

    lax.fori_loop(0, blocks, turn, 0)

    def factors(i, _):
        rows = pl.ds(pl.multiple_of(i * pdev, pdev), pdev)
        gain = jnp.broadcast_to(gain_ref[pl.ds(i, 1), :], (pdev, pdev)).T
        grow_ref[rows, :] = 1.0 + gain * wind_ref[...]
        damp_b[rows, :] = jnp.broadcast_to(damp_ref[pl.ds(i, 1), :], (pdev, pdev)).T
        return 0

    lax.fori_loop(0, blocks, factors, 0)

    acc_ref[...] = jnp.zeros_like(acc_ref)

    def place(j):
        for dy in range(yd):
            for c in range(2):
                src = 2 * chip_of(j, dy) + c
                cols = pl.ds((2 * dy + c) * pdev, pdev)
                rows = row_ref[j, :, cols].astype(F32)
                values = main_r1[src].astype(F32)
                for k in range(8):
                    lhs_ref[k * srows : (k + 1) * srows, cols] = (values[k : k + 1, :] * rows).astype(BF16)
                lhs_ref[8 * srows : 9 * srows, cols] = (last_r1[src] * rows).astype(BF16)
                lhs_ref[9 * srows :, cols] = (cls_ref[pl.ds(src, 1), :] * rows).astype(BF16)
        acc_ref[...] += nt(lhs_ref[...], col_ref[j])

    def arrived(sem, ref, count):
        pltpu.make_async_copy(ref.at[pl.ds(0, count)], ref.at[pl.ds(0, count)], sem).wait()

    def take(j, _):
        arrived(r1_sem.at[0, j], main_r1, 2 * yd)
        arrived(r1_sem.at[1, j], last_r1, 2 * yd)
        place(j)
        return 0

    lax.fori_loop(0, zd - 1, take, 0)
    arrived(r1_sem.at[0, zd - 1], main_r1, 2 * yd - 1)
    arrived(r1_sem.at[1, zd - 1], last_r1, 2 * yd - 1)
    place(zd - 1)

    sea = sea_ref[...].astype(F32)
    cell_class = acc_ref[9 * srows :, :]

    def comp_of(c):
        return 8 * me + c if c < 8 else whole + me

    def fluxes(c, top, count):
        comp = comp_of(c)
        freq = comp // NDIR
        energy = acc_ref[c * srows + top : c * srows + top + count, :] * sea[top : top + count]
        here = cell_class[top : top + count]
        speed = jnp.zeros_like(energy)
        for q in range(nclass):
            speed = jnp.where(here == float(q), table_ref[q, freq], speed)
        sx = speed * cos_ref[comp]
        sy = speed * sin_ref[comp]
        return energy, sx, sy

    edge = min(8, srows)
    for c in range(9):
        energy, sx, _ = fluxes(c, srows - edge, edge)
        halo_s[0, c : c + 1, :] = (jnp.maximum(sx, 0.0) * energy)[edge - 1 :, :]
        energy, sx, _ = fluxes(c, 0, edge)
        halo_s[1, c : c + 1, :] = (jnp.minimum(sx, 0.0) * energy)[:1, :]
    halo = [
        pltpu.make_async_remote_copy(
            src_ref=halo_s.at[k],
            dst_ref=halo_r.at[k],
            send_sem=halo_sem.at[0, k],
            recv_sem=halo_sem.at[1, k],
            device_id={"nest": peer},
            device_id_type=pl.DeviceIdType.MESH,
        )
        for k, peer in enumerate((nxt, prv))
    ]
    for copy in halo:
        copy.start()
    row_id = iota((srows, gy), 0)
    col_id = iota((srows, gy), 1)
    for c in range(9):
        energy, sx, sy = fluxes(c, 0, srows)
        plus_x = jnp.maximum(sx, 0.0) * energy
        minus_x = jnp.minimum(sx, 0.0) * energy
        plus_y = jnp.maximum(sy, 0.0) * energy
        minus_y = jnp.minimum(sy, 0.0) * energy
        inflow_x = jnp.where(row_id > 0, pltpu.roll(plus_x, 1, 0), 0.0) - jnp.where(
            row_id < srows - 1, pltpu.roll(minus_x, srows - 1, 0), 0.0
        )
        inflow_y = jnp.where(col_id > 0, pltpu.roll(plus_y, 1, 1), 0.0) - jnp.where(
            col_id < gy - 1, pltpu.roll(minus_y, gy - 1, 1), 0.0
        )
        adv_ref[c] = energy - (jnp.abs(sx) + jnp.abs(sy)) * energy + inflow_x + inflow_y
    for copy in halo:
        copy.wait()
    for c in range(9):
        from_prev = jnp.where(strip > 0, halo_r[0, c : c + 1, :], 0.0)
        from_next = jnp.where(strip < nnest - 1, halo_r[1, c : c + 1, :], 0.0)
        edges = jnp.where(row_id == 0, from_prev, 0.0) - jnp.where(row_id == srows - 1, from_next, 0.0)
        advb_ref[c * srows : (c + 1) * srows, :] = ((adv_ref[c] + edges) * sea).astype(BF16)

    def pick(cols, rows, count):
        found = nn(advb_ref[...], cols).reshape(9, srows, count)
        return jnp.sum(found * rows.astype(F32)[None], axis=1)

    at_list = pick(colb_ref[...], rowb_ref[...], NESTED * nc)
    padded = jnp.concatenate([at_list, jnp.zeros((7, NESTED * nc), F32)], axis=0)
    padded = jnp.concatenate([padded, padded, jnp.zeros((pdev - 32, NESTED * nc), F32)], axis=0).astype(BF16)
    half = [
        nt(onehot(iota((nc, NESTED * nc), 1) == NESTED * iota((nc, NESTED * nc), 0) + k), padded) for k in range(NESTED)
    ]
    bpt_ref[...] = jnp.where(iota((nc, pdev), 1) < 16, half[0], half[1])

    def second(dest, j):
        pltpu.make_async_remote_copy(
            src_ref=main_s2.at[dest],
            dst_ref=main_r2.at[me],
            send_sem=s2_sem.at[0],
            recv_sem=r2_sem.at[0, j],
            device_id={"comp": dest},
            device_id_type=pl.DeviceIdType.MESH,
        ).start()
        pltpu.make_async_remote_copy(
            src_ref=pair_s2.at[dest],
            dst_ref=pair_r2.at[me],
            send_sem=s2_sem.at[1],
            recv_sem=r2_sem.at[1, j],
            device_id={"comp": dest},
            device_id_type=pl.DeviceIdType.MESH,
        ).start()

    def give(j):
        for dy in range(yd):
            cols = pl.ds(dy * 2 * pdev, 2 * pdev)
            values = pick(col_ref[j, :, cols], row_ref[j, :, cols], 2 * pdev)
            for c in range(2):
                dest = 2 * chip_of(j, dy) + c
                mine = values[:, c * pdev : (c + 1) * pdev]
                main_s2[dest] = mine[:8].astype(BF16)
                pair_s2[dest] = jnp.concatenate([mine[8:], bpt_ref[pl.ds(dest, 1), :]], axis=0).astype(BF16)

    def give_group(j, _):
        give(j)
        for dy in range(yd):
            for c in range(2):
                second(2 * chip_of(j, dy) + c, mirror(j))
        return 0

    lax.fori_loop(0, zd - 1, give_group, 0)
    give(zd - 1)
    for dy in range(1, yd):
        for c in range(2):
            second(2 * chip_of(zd - 1, dy) + c, zd - 1)
    second(me + 1 - 2 * my_core, zd - 1)
    main_r2[me] = main_s2[me]
    pair_r2[me] = pair_s2[me]

    own = pl.ds(pl.multiple_of(my_core * pdev, pdev), pdev)
    at_slots = nn(sea.astype(BF16), col_ref[zd - 1, :, own]) * row_ref[zd - 1, :, own].astype(F32)
    live = jnp.sum(at_slots, axis=0, keepdims=True)

    def collect(j, _):
        arrived(r2_sem.at[0, j], main_r2, 2 * yd)
        arrived(r2_sem.at[1, j], pair_r2, 2 * yd)
        return 0

    lax.fori_loop(0, zd - 1, collect, 0)
    arrived(r2_sem.at[0, zd - 1], main_r2, 2 * yd - 1)
    arrived(r2_sem.at[1, zd - 1], pair_r2, 2 * yd - 1)
    total = jnp.zeros((8, pdev), F32)
    for i in range(nc // 2):
        upper = main_r2[2 * i].astype(F32)
        lower = main_r2[2 * i + 1].astype(F32)
        total = total + upper + lower
        prop_ref[16 * i : 16 * i + 16, :] = jnp.concatenate([upper, lower], axis=0).astype(BF16)
    for i in range(nc):
        pair = pair_r2[i].astype(F32)
        lastp_ref[i : i + 1, :] = pair[:1]
        listp_ref[i : i + 1, :] = pair[1:]
    prop_ref[whole:, :] = lastp_ref[...].astype(BF16)
    energy = (jnp.sum(total, axis=0, keepdims=True) + jnp.sum(lastp_ref[...], axis=0, keepdims=True)) / ncomp

    got = listp_ref[...].astype(BF16)
    wanted = iota((pdev, ncomp), 1)
    owner_row = jnp.where(wanted < whole, wanted // 8, wanted - whole)
    which = jnp.where(wanted < whole, wanted % 8, 8)
    for k in range(NESTED):
        spread = nn(got, onehot(iota((pdev, ncomp), 0) == 16 * k + which))
        keep = iota((nc, ncomp), 0) == owner_row[:nc]
        bnd_ref[k : k + 1, :] = jnp.sum(jnp.where(keep, spread, 0.0), axis=0, keepdims=True).astype(BF16)

    def cross(i, _):
        rows = pl.ds(pl.multiple_of(i * pdev, pdev), pdev)
        forward = nn(kern_ref[rows, :], prop_ref[...])
        backward = nn(kernt_ref[rows, :], prop_ref[...])
        cross_ref[rows, :] = (forward * backward).astype(BF16)
        return 0

    lax.fori_loop(0, blocks, cross, 0)

    def finish(i, _):
        rows = pl.ds(pl.multiple_of(i * pdev, pdev), pdev)
        coupling = nn(kern_ref[rows, :], cross_ref[...])
        growth = grow_ref[rows, :] - damp_b[rows, :] * energy
        value = jnp.maximum(prop_ref[rows, :].astype(F32) * growth + 0.1 * coupling, 0.0) * live
        upd_ref[rows, :] = value.astype(BF16)
        return 0

    lax.fori_loop(0, blocks, finish, 0)

    arrived(s1_sem.at[0], main_r1, nc - 1)
    arrived(s1_sem.at[1], last_r1, nc - 1)
    arrived(s2_sem.at[0], main_r2, nc - 1)
    arrived(s2_sem.at[1], pair_r2, nc - 1)


def body(
    spectra,
    kernel,
    wind_gain,
    damping,
    wind_speed,
    class_speed,
    depth_class,
    cell_of_point,
    sea_mask,
    bnd_owner,
    bnd_slot,
):
    ncomp, pdev = spectra.shape
    nc = lax.axis_size("comp")
    nnest = lax.axis_size("nest")
    srows, gy = sea_mask.shape
    nclass = class_speed.shape[0]
    blocks = ncomp // pdev
    angles = np.arange(NDIR, dtype=np.float32) * np.float32(2.0 * math.pi / NDIR)
    comp_dir = np.arange(ncomp) % NDIR
    cosines = jnp.asarray(np.cos(angles)[comp_dir], F32)
    sines = jnp.asarray(np.sin(angles)[comp_dir], F32)
    vmem, smem = pl.BlockSpec(memory_space=pltpu.VMEM), pl.BlockSpec(memory_space=pltpu.SMEM)
    sizes = (nc, ncomp, pdev, srows, gy, nclass, nnest)
    span = YDIM * 2 * pdev
    updated, boundary = pl.pallas_call(
        functools.partial(step_kernel, sizes),
        out_shape=(
            jax.ShapeDtypeStruct((ncomp, pdev), BF16),
            jax.ShapeDtypeStruct((NESTED, ncomp), BF16),
        ),
        in_specs=[vmem, pl.BlockSpec(memory_space=pl.ANY), vmem, vmem, vmem, smem, smem, smem] + [vmem] * 5,
        out_specs=(vmem, vmem),
        scratch_shapes=[
            pltpu.VMEM((nc, pdev), F32),
            pltpu.VMEM((nc, pdev), F32),
            pltpu.VMEM((nc, pdev), F32),
            pltpu.VMEM((ZDIM, gy, span), BF16),
            pltpu.VMEM((ZDIM, srows, span), BF16),
            pltpu.VMEM((gy, NESTED * nc), BF16),
            pltpu.VMEM((srows, NESTED * nc), BF16),
            pltpu.VMEM((10 * srows, span), BF16),
            pltpu.VMEM((10 * srows, gy), F32),
            pltpu.VMEM((9, srows, gy), F32),
            pltpu.VMEM((9 * srows, gy), BF16),
            pltpu.VMEM((nc, 1, pdev), F32),
            pltpu.VMEM((nc, 8, pdev), BF16),
            pltpu.VMEM((nc, 1, pdev), F32),
            pltpu.VMEM((nc, 8, pdev), BF16),
            pltpu.VMEM((nc, 2, pdev), BF16),
            pltpu.VMEM((nc, 8, pdev), BF16),
            pltpu.VMEM((nc, 2, pdev), BF16),
            pltpu.VMEM((nc, pdev), F32),
            pltpu.VMEM((nc, pdev), F32),
            pltpu.VMEM((nc, pdev), F32),
            pltpu.VMEM((2, 16, gy), F32),
            pltpu.VMEM((2, 16, gy), F32),
            pltpu.VMEM((ncomp, pdev), BF16),
            pltpu.VMEM((ncomp, ncomp), BF16),
            pltpu.VMEM((ncomp, ncomp), BF16),
            pltpu.VMEM((ncomp, pdev), F32),
            pltpu.VMEM((ncomp, pdev), F32),
            pltpu.VMEM((ncomp, pdev), BF16),
            pltpu.SemaphoreType.DMA,
            pltpu.SemaphoreType.DMA((2,)),
            pltpu.SemaphoreType.DMA((2, ZDIM)),
            pltpu.SemaphoreType.DMA((2,)),
            pltpu.SemaphoreType.DMA((2, ZDIM)),
            pltpu.SemaphoreType.DMA((2, 2)),
        ],
        compiler_params=pltpu.CompilerParams(collective_id=0, has_side_effects=True),
    )(
        spectra.reshape(ncomp // 8, 8, pdev),
        kernel,
        wind_gain.reshape(blocks, pdev),
        damping.reshape(blocks, pdev),
        wind_speed.reshape(1, pdev),
        class_speed,
        cosines,
        sines,
        depth_class.reshape(nc, pdev),
        cell_of_point.reshape(nc, pdev),
        sea_mask,
        bnd_owner,
        bnd_slot,
    )
    return updated, boundary[None]


def solution(mesh):
    placed = (
        P(None, ("nest", "comp")),
        P(),
        P(),
        P(),
        P(("nest", "comp")),
        P(),
        P("nest", None),
        P("nest", None),
        P("nest", None),
        P("nest", None),
        P("nest", None),
    )
    return jax.shard_map(
        body,
        mesh=mesh,
        in_specs=placed,
        out_specs=(P(None, ("nest", "comp")), P("nest", "comp", None)),
        check_vma=False,
    )
```

time: 308 us -> 76.9 us (0.25)
  local copies, waits for them, and re-layouts: 194 us -> 2.98 us
  Pallas kernels: 0 us -> 73.1 us
  starting transfers between devices: 49.4 us -> 0 us
  waiting for transfers between devices: 45.7 us -> 0 us
  other arithmetic: 9.96 us -> 0 us
  matrix products: 6.82 us -> 0 us
    scatter x2 -> x0, local copies, waits for them, and re-layouts: 105 us -> none  [the longest x1 60.6 us: body(): jnp.zeros((region_size,), jnp.int32).at[cell_ids].set(depth_class[0])]
    pallas_call x0 -> x1, Pallas kernels: none -> 73.1 us  [body(): pl.pallas_call(functools.partial(step_kernel, sizes), out_shape=(jax.Shap...]
    gather x6 -> x0, local copies, waits for them, and re-layouts: 68.7 us -> none  [the longest x2 61.9 us: body(): jnp.take(advected.reshape(per_device, region_size), cell_ids, axis=1)]
    all_to_all x3 -> x0, starting transfers between devices: 44.8 us -> none  [the longest x1 20.6 us: body(): lax.all_to_all(spectra, 'comp', split_axis=0, concat_axis=1, tiled=True)]
    all_to_all x3 -> x0, waiting for transfers between devices: 43.1 us -> none  [the longest x1 29.1 us: body(): lax.all_to_all(advected_points, 'comp', split_axis=1, concat_axis=0, tile...]
    all_to_all x7 -> x0, local copies, waits for them, and re-layouts: 8.17 us -> none  [the longest x3 5.47 us: body(): lax.all_to_all(spectra, 'comp', split_axis=0, concat_axis=1, tiled=True)]
    dot_general x4 -> x0, matrix products: 6.82 us -> none  [the longest x1 2.59 us: body(): coupling = jnp.dot(kernel, cross_terms, preferred_element_type=jnp.float32)]
    ppermute x2 -> x0, starting transfers between devices: 4.59 us -> none  [passed_along(): lax.ppermute(value, axis, [(source, source + steps) for source in range(i...]
  transfers between devices with their start and end apart: 5 -> 0, of which waited for: 3 -> 0; matrix products, arithmetic and copies ran while one was open for 25% -> 0% of each run, Pallas kernels for 0% -> 0%
where the time goes in v2:
time: 76.9 us; the launch traced here: 76.7 us
  Pallas kernels  73.1 us (95%)
  local copies, waits for them, and re-layouts  2.98 us (4%)
    pallas_call x1, Pallas kernels, body(): pl.pallas_call(functools.partial(step_kernel, sizes), out_shape=(jax.Shap...  73.1 us
    unnamed x2, local copies, waits for them, and re-layouts  2.98 us

profile of v2, /device:TPU:1, one launch (start us, length us, event | category | flops | bytes accessed | tf_op | source)
XLA Modules:
  0.0 76.7 jit_solution(18016025952935911774)
XLA Ops:
  0.6 73.1 %shard_map.140 = (bf16[1152,128]{1,0:T(8,128)(2,1)}, bf16[2,1152]{1,0:T(2,128)(2,1)}) custom-call(bf16[144,8,128]{2,1,0:T(8,128)(2,1)} %bitcast.7, bf16[1152,1152]{1,0:T(8,128)(2,1)} %kern_hbm.1, f32[9,128]{1,0:T(8,128)} %bitcast.10, f32[9,128]{1,0:T(8,128)} %bitcast.11, f32[1,128]{1,0:T(1,128)} %bitcast.13, f32[8,32]{1,0:T(8,128)} %table_ref.1, ...), custom_call_target="tpu_custom_call" | custom-call | tf_op jit(solution)/shard_map/pallas_call | solution.py:445
  73.7 1.7 %copy.17 = bf16[1152,128]{1,0:T(8,128)(2,1)} copy(bf16[1152,128]{1,0:T(8,128)(2,1)} %get-tuple-element.8) | data formatting | bytes 589824
  75.4 1.3 %copy.18 = bf16[1,2,1152]{2,1,0:T(2,128)(2,1)} copy(bf16[1,2,1152]{2,1,0:T(2,128)(2,1)} %bitcast.12) | data formatting | bytes 9216

commit v3 on v2

--- a/solution.py
+++ b/solution.py
@@ -33,8 +33,22 @@
 
 def step_kernel(
     sizes,
+    kern_hbm,
+    spec_hbm,
+    gain_hbm,
+    damp_hbm,
+    wind_hbm,
+    table_hbm,
+    cos_hbm,
+    sin_hbm,
+    class_hbm,
+    cell_hbm,
+    sea_hbm,
+    owner_hbm,
+    slot_hbm,
+    upd_ref,
+    bnd_ref,
     spec_ref,
-    kern_hbm,
     gain_ref,
     damp_ref,
     wind_ref,
@@ -46,8 +60,6 @@
     sea_ref,
     owner_ref,
     slot_ref,
-    upd_ref,
-    bnd_ref,
     lo_ref,
     hi_ref,
     cls_ref,
@@ -57,6 +69,7 @@
     rowb_ref,
     lhs_ref,
     acc_ref,
+    speed_ref,
     adv_ref,
     advb_ref,
     last_s,
@@ -78,6 +91,7 @@
     damp_b,
     cross_ref,
     kern_sem,
+    load_sem,
     s1_sem,
     r1_sem,
     s2_sem,
@@ -97,8 +111,16 @@
     prv = lax.rem(strip + nnest - 1, nnest)
 
     def offset(j):
-        odd = lax.rem(j, 2)
-        return zd // 2 + odd * ((j + 1) // 2) - (1 - odd) * (j // 2)
+        i = (j + 1) // 2
+        odd = lax.rem(i, 2)
+        far = odd * ((i + 1) // 2) + (1 - odd) * (zd // 2 - i // 2)
+        return lax.rem(zd + (1 - 2 * lax.rem(j, 2)) * far, zd) * (1 - j // (zd - 1))
+
+    def far_first(t):
+        far = zd // 2 - (t + 1) // 2
+        outer = far // (zd // 2 - (zd // 2 - 1) // 2)
+        i = outer * (zd - 2 * far) + (1 - outer) * (2 * far - 1)
+        return (2 * i - lax.rem(t, 2)) * ((t + zd - 1) // zd)
 
     def chip_of(j, dy):
         return lax.rem(my_y - dy + yd, yd) * zd + lax.rem(my_z - offset(j) + 2 * zd, zd)
@@ -111,18 +133,46 @@
         return j + odd * (1 - j // (zd - 1)) - (1 - odd) * ((j + zd - 1) // zd)
 
     kern_copy = pltpu.make_async_copy(kern_hbm, kern_ref, kern_sem)
+    held = (
+        (cell_hbm, cell_ref),
+        (spec_hbm, spec_ref),
+        (class_hbm, class_ref),
+        (gain_hbm, gain_ref),
+        (damp_hbm, damp_ref),
+        (wind_hbm, wind_ref),
+        (table_hbm, table_ref),
+        (cos_hbm, cos_ref),
+        (sin_hbm, sin_ref),
+        (sea_hbm, sea_ref),
+        (owner_hbm, owner_ref),
+        (slot_hbm, slot_ref),
+    )
+    loads = [pltpu.make_async_copy(far, near, load_sem.at[k]) for k, (far, near) in enumerate(held)]
+    for load in loads:
+        load.start()
     kern_copy.start()
 
     barrier = pltpu.get_barrier_semaphore()
 
-    def greet(i, _):
-        peer = lax.rem(me + i, nc)
-        pl.semaphore_signal(barrier, inc=1, device_id={"comp": peer}, device_id_type=pl.DeviceIdType.MESH)
-        return 0
-
-    lax.fori_loop(1, nc, greet, 0)
-    pl.semaphore_signal(barrier, inc=1, device_id={"nest": nxt}, device_id_type=pl.DeviceIdType.MESH)
-    pl.semaphore_signal(barrier, inc=1, device_id={"nest": prv}, device_id_type=pl.DeviceIdType.MESH)
+    def greet(peer):
+        pl.semaphore_signal(barrier, inc=1, device_id=peer, device_id_type=pl.DeviceIdType.MESH)
+
+    def greet_group(j, _):
+        for dy in range(yd):
+            for c in range(2):
+                greet({"comp": 2 * chip_to(j, dy) + c})
+        return 0
+
+    lax.fori_loop(0, zd - 1, greet_group, 0)
+    for dy in range(1, yd):
+        for c in range(2):
+            greet({"comp": 2 * chip_to(zd - 1, dy) + c})
+    greet({"comp": me + 1 - 2 * my_core})
+    greet({"nest": nxt})
+    greet({"nest": prv})
+
+    for load in loads:
+        load.wait()
 
     tail = spec_ref[nc:, :, :].astype(F32).reshape(ncomp - whole, pdev)
     last_s[...] = tail.reshape(ncomp - whole, 1, pdev)
@@ -170,11 +220,11 @@
                 first(2 * chip_to(j, dy) + c, j)
         return 0
 
-    lax.fori_loop(0, zd - 1, send_group, 0)
     for dy in range(1, yd):
         for c in range(2):
             first(2 * chip_to(zd - 1, dy) + c, zd - 1)
     first(me + 1 - 2 * my_core, zd - 1)
+    lax.fori_loop(0, zd - 1, send_group, 0)
     main_r1[me] = spec_ref[me]
     last_r1[me] = last_s[me]
 
@@ -190,27 +240,22 @@
     colb_ref[...] = onehot(iota((gy, NESTED * nc), 0).astype(F32) == listed(lo_ref))
     rowb_ref[...] = onehot(iota((srows, NESTED * nc), 0).astype(F32) == listed(hi_ref))
 
-    kern_copy.wait()
-    blocks = ncomp // pdev
-
-    def turn(i, _):
-        for k in range(blocks):
-            tile = kern_ref[pl.ds(pl.multiple_of(i * pdev, pdev), pdev), k * pdev : (k + 1) * pdev]
-            kernt_ref[k * pdev : (k + 1) * pdev, pl.ds(pl.multiple_of(i * pdev, pdev), pdev)] = (
-                tile.astype(F32).T.astype(BF16)
-            )
-        return 0
-
-    lax.fori_loop(0, blocks, turn, 0)
-
-    def factors(i, _):
-        rows = pl.ds(pl.multiple_of(i * pdev, pdev), pdev)
-        gain = jnp.broadcast_to(gain_ref[pl.ds(i, 1), :], (pdev, pdev)).T
-        grow_ref[rows, :] = 1.0 + gain * wind_ref[...]
-        damp_b[rows, :] = jnp.broadcast_to(damp_ref[pl.ds(i, 1), :], (pdev, pdev)).T
-        return 0
-
-    lax.fori_loop(0, blocks, factors, 0)
+    def place_class(j, total):
+        parts = []
+        for dy in range(yd):
+            for c in range(2):
+                cols = pl.ds((2 * dy + c) * pdev, pdev)
+                values = cls_ref[pl.ds(2 * chip_of(j, dy) + c, 1), :]
+                parts.append((values * row_ref[j, :, cols].astype(F32)).astype(BF16))
+        return total + nt(jnp.concatenate(parts, axis=1), col_ref[j])
+
+    cell_class = lax.fori_loop(0, zd, place_class, jnp.zeros((srows, gy), F32))
+    freqs = (8 * me // NDIR, (8 * me + 7) // NDIR, (whole + me) // NDIR)
+    for k, freq in enumerate(freqs):
+        speed = jnp.zeros((srows, gy), F32)
+        for q in range(nclass):
+            speed = jnp.where(cell_class == float(q), table_ref[q, freq], speed)
+        speed_ref[k] = speed
 
     acc_ref[...] = jnp.zeros_like(acc_ref)
 
@@ -219,42 +264,44 @@
             for c in range(2):
                 src = 2 * chip_of(j, dy) + c
                 cols = pl.ds((2 * dy + c) * pdev, pdev)
-                rows = row_ref[j, :, cols].astype(F32)
+                rows = row_ref[j, :, cols]
                 values = main_r1[src].astype(F32)
-                for k in range(8):
-                    lhs_ref[k * srows : (k + 1) * srows, cols] = (values[k : k + 1, :] * rows).astype(BF16)
-                lhs_ref[8 * srows : 9 * srows, cols] = (last_r1[src] * rows).astype(BF16)
-                lhs_ref[9 * srows :, cols] = (cls_ref[pl.ds(src, 1), :] * rows).astype(BF16)
+                for k in range(9):
+                    value = values[k : k + 1, :] if k < 8 else last_r1[src]
+                    if srows % 16 == 0:
+                        value = jnp.broadcast_to(value, (16, pdev)).astype(BF16)
+                        placed = (rows.reshape(srows // 16, 16, pdev) * value[None]).reshape(srows, pdev)
+                    else:
+                        placed = rows * value.astype(BF16)
+                    lhs_ref[k * srows : (k + 1) * srows, cols] = placed
         acc_ref[...] += nt(lhs_ref[...], col_ref[j])
 
     def arrived(sem, ref, count):
         pltpu.make_async_copy(ref.at[pl.ds(0, count)], ref.at[pl.ds(0, count)], sem).wait()
 
-    def take(j, _):
+    arrived(r1_sem.at[0, zd - 1], main_r1, 2 * yd - 1)
+    arrived(r1_sem.at[1, zd - 1], last_r1, 2 * yd - 1)
+    place(zd - 1)
+
+    def take(t, _):
+        j = lax.rem(t + 1, zd - 1)
         arrived(r1_sem.at[0, j], main_r1, 2 * yd)
         arrived(r1_sem.at[1, j], last_r1, 2 * yd)
         place(j)
         return 0
 
     lax.fori_loop(0, zd - 1, take, 0)
-    arrived(r1_sem.at[0, zd - 1], main_r1, 2 * yd - 1)
-    arrived(r1_sem.at[1, zd - 1], last_r1, 2 * yd - 1)
-    place(zd - 1)
 
     sea = sea_ref[...].astype(F32)
-    cell_class = acc_ref[9 * srows :, :]
 
     def comp_of(c):
         return 8 * me + c if c < 8 else whole + me
 
     def fluxes(c, top, count):
         comp = comp_of(c)
-        freq = comp // NDIR
+        which = comp // NDIR - freqs[0] if c < 8 else 2
         energy = acc_ref[c * srows + top : c * srows + top + count, :] * sea[top : top + count]
-        here = cell_class[top : top + count]
-        speed = jnp.zeros_like(energy)
-        for q in range(nclass):
-            speed = jnp.where(here == float(q), table_ref[q, freq], speed)
+        speed = speed_ref[which, top : top + count, :]
         sx = speed * cos_ref[comp]
         sy = speed * sin_ref[comp]
         return energy, sx, sy
@@ -341,7 +388,8 @@
                 main_s2[dest] = mine[:8].astype(BF16)
                 pair_s2[dest] = jnp.concatenate([mine[8:], bpt_ref[pl.ds(dest, 1), :]], axis=0).astype(BF16)
 
-    def give_group(j, _):
+    def give_group(t, _):
+        j = far_first(t)
         give(j)
         for dy in range(yd):
             for c in range(2):
@@ -361,24 +409,51 @@
     at_slots = nn(sea.astype(BF16), col_ref[zd - 1, :, own]) * row_ref[zd - 1, :, own].astype(F32)
     live = jnp.sum(at_slots, axis=0, keepdims=True)
 
-    def collect(j, _):
+    kern_copy.wait()
+    blocks = ncomp // pdev
+
+    def turn(i, _):
+        for k in range(blocks):
+            tile = kern_ref[pl.ds(pl.multiple_of(i * pdev, pdev), pdev), k * pdev : (k + 1) * pdev]
+            kernt_ref[k * pdev : (k + 1) * pdev, pl.ds(pl.multiple_of(i * pdev, pdev), pdev)] = (
+                tile.T
+            )
+        return 0
+
+    lax.fori_loop(0, blocks, turn, 0)
+
+    def factors(i, _):
+        rows = pl.ds(pl.multiple_of(i * pdev, pdev), pdev)
+        gain = jnp.broadcast_to(gain_ref[pl.ds(i, 1), :], (pdev, pdev)).T
+        grow_ref[rows, :] = 1.0 + gain * wind_ref[...]
+        damp_b[rows, :] = jnp.broadcast_to(damp_ref[pl.ds(i, 1), :], (pdev, pdev)).T
+        return 0
+
+    lax.fori_loop(0, blocks, factors, 0)
+
+    def gather(j, total):
+        for dy in range(yd):
+            chip = chip_of(j, dy)
+            upper = main_r2[2 * chip].astype(F32)
+            lower = main_r2[2 * chip + 1].astype(F32)
+            total = total + (upper + lower)
+            prop_ref[pl.ds(pl.multiple_of(16 * chip, 16), 16), :] = jnp.concatenate([upper, lower], axis=0).astype(BF16)
+            for c in range(2):
+                pair = pair_r2[2 * chip + c].astype(F32)
+                lastp_ref[pl.ds(2 * chip + c, 1), :] = pair[:1]
+                listp_ref[pl.ds(2 * chip + c, 1), :] = pair[1:]
+        return total
+
+    def collect(t, total):
+        j = far_first(t)
         arrived(r2_sem.at[0, j], main_r2, 2 * yd)
         arrived(r2_sem.at[1, j], pair_r2, 2 * yd)
-        return 0
-
-    lax.fori_loop(0, zd - 1, collect, 0)
+        return gather(j, total)
+
+    total = lax.fori_loop(0, zd - 1, collect, jnp.zeros((8, pdev), F32))
     arrived(r2_sem.at[0, zd - 1], main_r2, 2 * yd - 1)
     arrived(r2_sem.at[1, zd - 1], pair_r2, 2 * yd - 1)
-    total = jnp.zeros((8, pdev), F32)
-    for i in range(nc // 2):
-        upper = main_r2[2 * i].astype(F32)
-        lower = main_r2[2 * i + 1].astype(F32)
-        total = total + upper + lower
-        prop_ref[16 * i : 16 * i + 16, :] = jnp.concatenate([upper, lower], axis=0).astype(BF16)
-    for i in range(nc):
-        pair = pair_r2[i].astype(F32)
-        lastp_ref[i : i + 1, :] = pair[:1]
-        listp_ref[i : i + 1, :] = pair[1:]
+    total = gather(zd - 1, total)
     prop_ref[whole:, :] = lastp_ref[...].astype(BF16)
     energy = (jnp.sum(total, axis=0, keepdims=True) + jnp.sum(lastp_ref[...], axis=0, keepdims=True)) / ncomp
 
@@ -391,24 +466,26 @@
         keep = iota((nc, ncomp), 0) == owner_row[:nc]
         bnd_ref[k : k + 1, :] = jnp.sum(jnp.where(keep, spread, 0.0), axis=0, keepdims=True).astype(BF16)
 
+    big = 3 * pdev if blocks % 3 == 0 else pdev
+
     def cross(i, _):
-        rows = pl.ds(pl.multiple_of(i * pdev, pdev), pdev)
+        rows = pl.ds(pl.multiple_of(i * big, big), big)
         forward = nn(kern_ref[rows, :], prop_ref[...])
         backward = nn(kernt_ref[rows, :], prop_ref[...])
         cross_ref[rows, :] = (forward * backward).astype(BF16)
         return 0
 
-    lax.fori_loop(0, blocks, cross, 0)
+    lax.fori_loop(0, ncomp // big, cross, 0)
 
     def finish(i, _):
-        rows = pl.ds(pl.multiple_of(i * pdev, pdev), pdev)
+        rows = pl.ds(pl.multiple_of(i * big, big), big)
         coupling = nn(kern_ref[rows, :], cross_ref[...])
         growth = grow_ref[rows, :] - damp_b[rows, :] * energy
         value = jnp.maximum(prop_ref[rows, :].astype(F32) * growth + 0.1 * coupling, 0.0) * live
         upd_ref[rows, :] = value.astype(BF16)
         return 0
 
-    lax.fori_loop(0, blocks, finish, 0)
+    lax.fori_loop(0, ncomp // big, finish, 0)
 
     arrived(s1_sem.at[0], main_r1, nc - 1)
     arrived(s1_sem.at[1], last_r1, nc - 1)
@@ -439,7 +516,7 @@
     comp_dir = np.arange(ncomp) % NDIR
     cosines = jnp.asarray(np.cos(angles)[comp_dir], F32)
     sines = jnp.asarray(np.sin(angles)[comp_dir], F32)
-    vmem, smem = pl.BlockSpec(memory_space=pltpu.VMEM), pl.BlockSpec(memory_space=pltpu.SMEM)
+    vmem = pl.BlockSpec(memory_space=pltpu.VMEM)
     sizes = (nc, ncomp, pdev, srows, gy, nclass, nnest)
     span = YDIM * 2 * pdev
     updated, boundary = pl.pallas_call(
@@ -448,9 +525,21 @@
             jax.ShapeDtypeStruct((ncomp, pdev), BF16),
             jax.ShapeDtypeStruct((NESTED, ncomp), BF16),
         ),
-        in_specs=[vmem, pl.BlockSpec(memory_space=pl.ANY), vmem, vmem, vmem, smem, smem, smem] + [vmem] * 5,
+        in_specs=[pl.BlockSpec(memory_space=pl.ANY)] * 13,
         out_specs=(vmem, vmem),
         scratch_shapes=[
+            pltpu.VMEM((ncomp // 8, 8, pdev), BF16),
+            pltpu.VMEM((blocks, pdev), F32),
+            pltpu.VMEM((blocks, pdev), F32),
+            pltpu.VMEM((1, pdev), F32),
+            pltpu.SMEM(class_speed.shape, F32),
+            pltpu.SMEM((ncomp,), F32),
+            pltpu.SMEM((ncomp,), F32),
+            pltpu.VMEM((nc, pdev), I32),
+            pltpu.VMEM((nc, pdev), I32),
+            pltpu.VMEM((srows, gy), I32),
+            pltpu.VMEM((1, NESTED * nc), I32),
+            pltpu.VMEM((1, NESTED * nc), I32),
             pltpu.VMEM((nc, pdev), F32),
             pltpu.VMEM((nc, pdev), F32),
             pltpu.VMEM((nc, pdev), F32),
@@ -458,8 +547,9 @@
             pltpu.VMEM((ZDIM, srows, span), BF16),
             pltpu.VMEM((gy, NESTED * nc), BF16),
             pltpu.VMEM((srows, NESTED * nc), BF16),
-            pltpu.VMEM((10 * srows, span), BF16),
-            pltpu.VMEM((10 * srows, gy), F32),
+            pltpu.VMEM((9 * srows, span), BF16),
+            pltpu.VMEM((9 * srows, gy), F32),
+            pltpu.VMEM((3, srows, gy), F32),
             pltpu.VMEM((9, srows, gy), F32),
             pltpu.VMEM((9 * srows, gy), BF16),
             pltpu.VMEM((nc, 1, pdev), F32),
@@ -481,6 +571,7 @@
             pltpu.VMEM((ncomp, pdev), F32),
             pltpu.VMEM((ncomp, pdev), BF16),
             pltpu.SemaphoreType.DMA,
+            pltpu.SemaphoreType.DMA((12,)),
             pltpu.SemaphoreType.DMA((2,)),
             pltpu.SemaphoreType.DMA((2, ZDIM)),
             pltpu.SemaphoreType.DMA((2,)),
@@ -489,8 +580,8 @@
         ],
         compiler_params=pltpu.CompilerParams(collective_id=0, has_side_effects=True),
     )(
+        kernel,
         spectra.reshape(ncomp // 8, 8, pdev),
-        kernel,
         wind_gain.reshape(blocks, pdev),
         damping.reshape(blocks, pdev),
         wind_speed.reshape(1, pdev),

time: 76.9 us -> 71.5 us (0.930)
  Pallas kernels: 73.1 us -> 67.6 us
    pallas_call x1, Pallas kernels: 73.1 us -> 67.6 us  [body(): pl.pallas_call(functools.partial(step_kernel, sizes), out_shape=(jax.Shap...]
where the time goes in v3:
time: 71.5 us; the launch traced here: 71.3 us
  Pallas kernels  67.6 us (95%)
  local copies, waits for them, and re-layouts  2.98 us (4%)
    pallas_call x1, Pallas kernels, body(): pl.pallas_call(functools.partial(step_kernel, sizes), out_shape=(jax.Shap...  67.6 us
    unnamed x2, local copies, waits for them, and re-layouts  2.98 us

profile of v3, /device:TPU:1, one launch (start us, length us, event | category | flops | bytes accessed | tf_op | source)
XLA Modules:
  0.0 71.3 jit_solution(2298434489166907348)
XLA Ops:
  0.6 67.6 %shard_map.140 = (bf16[1152,128]{1,0:T(8,128)(2,1)}, bf16[2,1152]{1,0:T(2,128)(2,1)}) custom-call(bf16[1152,1152]{1,0:T(8,128)(2,1)} %kern_hbm.1, bf16[144,8,128]{2,1,0:T(8,128)(2,1)} %bitcast.7, f32[9,128]{1,0:T(8,128)} %bitcast.10, f32[9,128]{1,0:T(8,128)} %bitcast.11, f32[1,128]{1,0:T(1,128)} %bitcast.13, f32[8,32]{1,0:T(8,128)} %table_hbm.1, ...), custom_call_target="tpu_custom_call" | custom-call | tf_op jit(solution)/shard_map/pallas_call | solution.py:522
  68.3 1.7 %copy.17 = bf16[1152,128]{1,0:T(8,128)(2,1)} copy(bf16[1152,128]{1,0:T(8,128)(2,1)} %get-tuple-element.8) | data formatting | bytes 589824
  70.0 1.3 %copy.18 = bf16[1,2,1152]{2,1,0:T(2,128)(2,1)} copy(bf16[1,2,1152]{2,1,0:T(2,128)(2,1)} %bitcast.12) | data formatting | bytes 9216

commit v4 on v3

--- a/solution.py
+++ b/solution.py
@@ -76,9 +76,7 @@
     main_r1,
     last_r1,
     main_s2,
-    pair_s2,
     main_r2,
-    pair_r2,
     bpt_ref,
     lastp_ref,
     listp_ref,
@@ -364,19 +362,11 @@
         pltpu.make_async_remote_copy(
             src_ref=main_s2.at[dest],
             dst_ref=main_r2.at[me],
-            send_sem=s2_sem.at[0],
-            recv_sem=r2_sem.at[0, j],
+            send_sem=s2_sem,
+            recv_sem=r2_sem.at[j],
             device_id={"comp": dest},
             device_id_type=pl.DeviceIdType.MESH,
         ).start()
-        pltpu.make_async_remote_copy(
-            src_ref=pair_s2.at[dest],
-            dst_ref=pair_r2.at[me],
-            send_sem=s2_sem.at[1],
-            recv_sem=r2_sem.at[1, j],
-            device_id={"comp": dest},
-            device_id_type=pl.DeviceIdType.MESH,
-        ).start()
 
     def give(j):
         for dy in range(yd):
@@ -385,8 +375,10 @@
             for c in range(2):
                 dest = 2 * chip_of(j, dy) + c
                 mine = values[:, c * pdev : (c + 1) * pdev]
-                main_s2[dest] = mine[:8].astype(BF16)
-                pair_s2[dest] = jnp.concatenate([mine[8:], bpt_ref[pl.ds(dest, 1), :]], axis=0).astype(BF16)
+                listed_row = bpt_ref[pl.ds(dest, 1), :]
+                for k in range(5):
+                    two = mine[2 * k : 2 * k + 2] if k < 4 else jnp.concatenate([mine[8:], listed_row], axis=0)
+                    main_s2[dest, k] = two.astype(BF16)
 
     def give_group(t, _):
         j = far_first(t)
@@ -403,7 +395,6 @@
             second(2 * chip_of(zd - 1, dy) + c, zd - 1)
     second(me + 1 - 2 * my_core, zd - 1)
     main_r2[me] = main_s2[me]
-    pair_r2[me] = pair_s2[me]
 
     own = pl.ds(pl.multiple_of(my_core * pdev, pdev), pdev)
     at_slots = nn(sea.astype(BF16), col_ref[zd - 1, :, own]) * row_ref[zd - 1, :, own].astype(F32)
@@ -434,25 +425,24 @@
     def gather(j, total):
         for dy in range(yd):
             chip = chip_of(j, dy)
-            upper = main_r2[2 * chip].astype(F32)
-            lower = main_r2[2 * chip + 1].astype(F32)
+            upper, lower = (
+                jnp.concatenate([main_r2[2 * chip + c, k].astype(F32) for k in range(4)], axis=0) for c in range(2)
+            )
             total = total + (upper + lower)
             prop_ref[pl.ds(pl.multiple_of(16 * chip, 16), 16), :] = jnp.concatenate([upper, lower], axis=0).astype(BF16)
             for c in range(2):
-                pair = pair_r2[2 * chip + c].astype(F32)
+                pair = main_r2[2 * chip + c, 4].astype(F32)
                 lastp_ref[pl.ds(2 * chip + c, 1), :] = pair[:1]
                 listp_ref[pl.ds(2 * chip + c, 1), :] = pair[1:]
         return total
 
     def collect(t, total):
         j = far_first(t)
-        arrived(r2_sem.at[0, j], main_r2, 2 * yd)
-        arrived(r2_sem.at[1, j], pair_r2, 2 * yd)
+        arrived(r2_sem.at[j], main_r2, 2 * yd)
         return gather(j, total)
 
     total = lax.fori_loop(0, zd - 1, collect, jnp.zeros((8, pdev), F32))
-    arrived(r2_sem.at[0, zd - 1], main_r2, 2 * yd - 1)
-    arrived(r2_sem.at[1, zd - 1], pair_r2, 2 * yd - 1)
+    arrived(r2_sem.at[zd - 1], main_r2, 2 * yd - 1)
     total = gather(zd - 1, total)
     prop_ref[whole:, :] = lastp_ref[...].astype(BF16)
     energy = (jnp.sum(total, axis=0, keepdims=True) + jnp.sum(lastp_ref[...], axis=0, keepdims=True)) / ncomp
@@ -489,8 +479,7 @@
 
     arrived(s1_sem.at[0], main_r1, nc - 1)
     arrived(s1_sem.at[1], last_r1, nc - 1)
-    arrived(s2_sem.at[0], main_r2, nc - 1)
-    arrived(s2_sem.at[1], pair_r2, nc - 1)
+    arrived(s2_sem, main_r2, nc - 1)
 
 
 def body(
@@ -555,10 +544,8 @@
             pltpu.VMEM((nc, 1, pdev), F32),
             pltpu.VMEM((nc, 8, pdev), BF16),
             pltpu.VMEM((nc, 1, pdev), F32),
-            pltpu.VMEM((nc, 8, pdev), BF16),
-            pltpu.VMEM((nc, 2, pdev), BF16),
-            pltpu.VMEM((nc, 8, pdev), BF16),
-            pltpu.VMEM((nc, 2, pdev), BF16),
+            pltpu.VMEM((nc, 5, 2, pdev), BF16),
+            pltpu.VMEM((nc, 5, 2, pdev), BF16),
             pltpu.VMEM((nc, pdev), F32),
             pltpu.VMEM((nc, pdev), F32),
             pltpu.VMEM((nc, pdev), F32),
@@ -574,8 +561,8 @@
             pltpu.SemaphoreType.DMA((12,)),
             pltpu.SemaphoreType.DMA((2,)),
             pltpu.SemaphoreType.DMA((2, ZDIM)),
-            pltpu.SemaphoreType.DMA((2,)),
-            pltpu.SemaphoreType.DMA((2, ZDIM)),
+            pltpu.SemaphoreType.DMA,
+            pltpu.SemaphoreType.DMA((ZDIM,)),
             pltpu.SemaphoreType.DMA((2, 2)),
         ],
         compiler_params=pltpu.CompilerParams(collective_id=0, has_side_effects=True),

time: 71.5 us -> 71.3 us (level)
  no operation moved by 1% of the time
where the time goes in v4:
time: 71.3 us; the launch traced here: 71.1 us
  Pallas kernels  67.5 us (95%)
  local copies, waits for them, and re-layouts  2.98 us (4%)
    pallas_call x1, Pallas kernels, body(): pl.pallas_call(functools.partial(step_kernel, sizes), out_shape=(jax.Shap...  67.5 us
    unnamed x2, local copies, waits for them, and re-layouts  2.98 us

profile of v4, /device:TPU:1, one launch (start us, length us, event | category | flops | bytes accessed | tf_op | source)
XLA Modules:
  0.0 71.1 jit_solution(15833962646728106360)
XLA Ops:
  0.6 67.5 %shard_map.140 = (bf16[1152,128]{1,0:T(8,128)(2,1)}, bf16[2,1152]{1,0:T(2,128)(2,1)}) custom-call(bf16[1152,1152]{1,0:T(8,128)(2,1)} %kern_hbm.1, bf16[144,8,128]{2,1,0:T(8,128)(2,1)} %bitcast.7, f32[9,128]{1,0:T(8,128)} %bitcast.10, f32[9,128]{1,0:T(8,128)} %bitcast.11, f32[1,128]{1,0:T(1,128)} %bitcast.13, f32[8,32]{1,0:T(8,128)} %table_hbm.1, ...), custom_call_target="tpu_custom_call" | custom-call | tf_op jit(solution)/shard_map/pallas_call | solution.py:511
  68.1 1.7 %copy.17 = bf16[1152,128]{1,0:T(8,128)(2,1)} copy(bf16[1152,128]{1,0:T(8,128)(2,1)} %get-tuple-element.8) | data formatting | bytes 589824
  69.8 1.3 %copy.18 = bf16[1,2,1152]{2,1,0:T(2,128)(2,1)} copy(bf16[1,2,1152]{2,1,0:T(2,128)(2,1)} %bitcast.12) | data formatting | bytes 9216
